TPU v7x, 32 devices: a whole 2x2x4 slice. The times are simulated.
32 devices in a mesh: wide: 16 (over z, y, core), shard: 2 (over x).
Axes of the slice: x: 2, y: 2, z: 4, core: 2. Of those that a mesh axis runs over, the one named last changes fastest.
Arguments:
- weights: bfloat16 [256, 8192], P('shard'), may hold values from -6 to 6
- momentum: bfloat16 [16, 256, 8192], P('wide', 'shard'), may hold values from -6 to 6
- grads: bfloat16 [2, 16, 256, 8192], P(None, 'wide', 'shard'), may hold values from -6 to 6
- offsets: int32 [2, 64], P('shard'), may hold values from 0 to 96
- owners: int32 [2, 64], P('shard'), may hold values from 0 to 63, each once within a row
- exp_avg: float32 [2, 64, 32, 128], P('shard', 'wide'), may hold values from -7 to 7
- exp_sq: float32 [2, 64, 32, 128], P('shard', 'wide'), may hold values from 0.01 to 1
Outputs:
- new_weights: bfloat16 [256, 8192], P('shard')
- new_momentum: bfloat16 [16, 256, 8192], P('wide', 'shard')
- new_avg: float32 [2, 64, 32, 128], P('shard', 'wide')
- new_sq: float32 [2, 64, 32, 128], P('shard', 'wide')
- scales: float32 [2], replicated
Inputs may be any that keep to these rules, and one draw needn't show every extreme that they name: `offsets`: each block's band spans 32 consecutive transform rows. Each row of owners is a permutation of 0 to 63.
All inputs are finite; a program needn't handle non-finite values.
Results may differ from a plain program's by a relative error of at most 0.003.
Values may be sent and summed in bfloat16 or wider, within the bound.
No kernel may reach another device: no remote copies, remote signals or barrier semaphores. Data moves between devices by JAX's collectives and lax.ppermute only.
A program may use at most 128 MiB of HBM per device.

v0:
```python
import jax
import jax.numpy as jnp
from jax import lax
from jax.sharding import PartitionSpec as P

STEPS = 2
highest = lax.Precision.HIGHEST
momentum_decay = 0.9
beta_one = 0.8
beta_two = 0.95
adam_eps = 1e-08
rms_eps = 1e-06
learning_rate = 0.2


def dct_table(length):
    frequency = jnp.arange(length, dtype=jnp.float32)[:, None]
    position = jnp.arange(length, dtype=jnp.float32)[None, :]
    cosines = jnp.cos(jnp.pi * (2.0 * position + 1.0) * frequency / (2.0 * length))
    scaling = jnp.where(frequency == 0.0, jnp.sqrt(1.0 / length), jnp.sqrt(2.0 / length))
    return cosines * scaling


def band_tables(basis, offsets, band_rows):
    indices = offsets[:, :, None] + jnp.arange(band_rows, dtype=jnp.int32)[None, None, :]
    return basis[indices]


def inverse(coefs, picked, basis):
    right_part = jnp.einsum("rjpc,cb->rjpb", coefs, basis, precision=highest)
    return jnp.einsum("rjpa,rjpb->rajb", picked, right_part, precision=highest)


def per_device(weights, momentum, grads, offsets, owners, exp_avg, exp_sq):
    block_len = exp_avg.shape[3]
    band_rows = exp_avg.shape[2]
    basis = dct_table(block_len)
    picked = band_tables(basis, offsets, band_rows)
    slot_order = jnp.argsort(owners, axis=1)
    row_blocks = offsets.shape[0]
    col_blocks = offsets.shape[1]
    block_shape = (row_blocks, block_len, col_blocks, block_len)
    replicas = lax.axis_size("wide")
    count_all = exp_avg.size * lax.axis_size("wide") * lax.axis_size("shard")
    weight_now = weights.astype(jnp.float32).reshape(block_shape)
    moment_now = momentum[0].astype(jnp.float32).reshape(block_shape)
    avg_now = exp_avg
    sq_now = exp_sq
    scales = []
    for step_index in range(STEPS):
        blended = momentum_decay * moment_now + grads[step_index, 0].astype(jnp.float32).reshape(
            block_shape
        )
        left_part = jnp.einsum("rjpa,rajb->rjpb", picked, blended, precision=highest)
        band_coef = jnp.einsum("rjpb,cb->rjpc", left_part, basis, precision=highest)
        moment_now = blended - inverse(band_coef, picked, basis)
        slot_band = jnp.take_along_axis(band_coef, slot_order[:, :, None, None], axis=1)
        pieces = lax.all_to_all(
            slot_band.astype(jnp.bfloat16), "wide", split_axis=1, concat_axis=0, tiled=True
        ).astype(slot_band.dtype)
        summed = jnp.sum(pieces.reshape((replicas, row_blocks) + pieces.shape[1:]), axis=0)
        mean_band = summed / replicas
        avg_now = beta_one * avg_now + (1.0 - beta_one) * mean_band
        sq_now = beta_two * sq_now + (1.0 - beta_two) * mean_band * mean_band
        raw_update = avg_now / (jnp.sqrt(sq_now) + adam_eps)
        power_sum = lax.psum(jnp.sum(raw_update * raw_update), ("wide", "shard"))
        spread = jnp.sqrt(power_sum / count_all + rms_eps)
        update = (raw_update / spread).astype(jnp.bfloat16)
        gathered = lax.all_gather(update, "wide", axis=1, tiled=True)
        block_update = jnp.take_along_axis(
            gathered.astype(jnp.float32), owners[:, :, None, None], axis=1
        )
        weight_now = weight_now - learning_rate * inverse(block_update, picked, basis)
        scales.append(spread)
    new_weights = weight_now.reshape(weights.shape).astype(jnp.bfloat16)
    new_momentum = moment_now.reshape(momentum.shape).astype(jnp.bfloat16)
    return (new_weights, new_momentum, avg_now, sq_now, jnp.stack(scales))


def solution(mesh):
    in_specs = (
        P("shard", None),
        P("wide", "shard", None),
        P(None, "wide", "shard", None),
        P("shard", None),
        P("shard", None),
        P("shard", "wide", None, None),
        P("shard", "wide", None, None),
    )
    out_specs = (
        P("shard", None),
        P("wide", "shard", None),
        P("shard", "wide", None, None),
        P("shard", "wide", None, None),
        P(),
    )
    return jax.shard_map(
        per_device, mesh=mesh, in_specs=in_specs, out_specs=out_specs, check_vma=False
    )
```

profile of v0, /device:TPU:0, one launch (start us, length us, event | category | flops | bytes accessed | tf_op | source)
XLA Modules:
  0.0 231.6 jit_solution(10638912373604838056)
XLA Ops:
  3.4 6.6 %slice_convert_fusion.1 = (f32[1,1,128,8192]{3,2,1,0:T(8,128)}, f32[16,8,64,128]{3,1,2,0:T(8,128)S(1)}, f32[1,1,128,8192]{3,2,1,0:T(8,128)}) fusion(bf16[2,1,128,8192]{3,2,1,0:T(8,128)(2,1)} %param.11), kind=kLoop, calls=%fused_computation.20 | loop fusion | flops 2097152 | bytes 16777216 | tf_op jit(solution)/shard_map/convert_element_type | solution.py:51
  10.0 2.7 %copy.56 = f32[16,8,64,128]{3,2,1,0:T(8,128)} copy(f32[16,8,64,128]{3,1,2,0:T(8,128)S(1)} %get-tuple-element.34) | data formatting | bytes 8388608
  12.7 2.5 %convert_multiply_fusion = (f32[1,128,8192]{2,1,0:T(8,128)}, f32[16,8,64,128]{3,1,2,0:T(8,128)S(1)}) fusion(bf16[1,128,8192]{2,1,0:T(8,128)(2,1)S(1)} %copy-done.2), kind=kLoop, calls=%fused_computation.18 | loop fusion | flops 2097152 | bytes 10485760 | tf_op jit(solution)/shard_map/mul | solution.py:51
  15.3 2.7 %copy.55 = f32[16,8,64,128]{3,2,1,0:T(8,128)} copy(f32[16,8,64,128]{3,1,2,0:T(8,128)S(1)} %get-tuple-element.37) | data formatting | bytes 8388608
  18.2 6.0 %gather_fusion = f32[2048,128]{1,0:T(8,128)S(1)} fusion(f32[128,128]{1,0:T(8,128)S(1)} %cosine_multiply_fusion, s32[2048]{0:T(1024)S(1)} %broadcast_clamp_fusion), kind=kCustom, calls=%fused_computation.4 | custom fusion | bytes 2105344 | tf_op jit(solution)/shard_map/gather | solution.py:26
  24.2 12.7 %fusion.6 = f32[64,32,128]{2,1,0:T(8,128)S(1)} fusion(f32[64,32,128]{2,1,0:T(8,128)S(1)} %bitcast.197, f32[128,64,128]{2,1,0:T(8,128)} %bitcast.204, f32[128,64,128]{2,1,0:T(8,128)} %bitcast.205), kind=kOutput, calls=%fused_computation.16 | convolution fusion | flops 403701760 | bytes 10485760 | tf_op jit(solution)/shard_map/rjpa,rajb->rjpb/dot_general | solution.py:54
  36.9 1.2 fusion.30
  38.1 1.2 fusion.27
  39.3 5.6 %copy.44 = f32[1,1,128,8192]{2,3,1,0:T(8,128)} copy(f32[1,1,128,8192]{3,2,1,0:T(8,128)} %get-tuple-element.33) | data formatting | bytes 8388608 | tf_op jit(solution)/shard_map/convert_element_type | solution.py:51
  44.9 5.6 %copy.45 = f32[1,1,128,8192]{2,3,1,0:T(8,128)} copy(f32[1,1,128,8192]{3,2,1,0:T(8,128)} %get-tuple-element.35) | data formatting | bytes 8388608 | tf_op jit(solution)/shard_map/convert_element_type | solution.py:51
  50.5 5.6 %copy.43 = f32[1,128,8192]{1,2,0:T(8,128)} copy(f32[1,128,8192]{2,1,0:T(8,128)} %get-tuple-element.36) | data formatting | bytes 8388608 | tf_op jit(solution)/shard_map/mul | solution.py:51
  56.1 10.1 %fusion.3 = f32[1,128,64,128]{1,3,2,0:T(8,128)S(1)} fusion(f32[1,128,64,128]{1,3,2,0:T(8,128)} %bitcast.207, f32[1,128,64,128]{1,3,2,0:T(8,128)} %bitcast.208, f32[1,128,64,128]{1,3,2,0:T(8,128)} %bitcast.206, f32[64,32,128]{2,1,0:T(8,128)S(1)} %fusion.27, f32[64,32,128]{2,1,0:T(8,128)S(1)} %bitcast.198), kind=kOutput, calls=%fused_computation.11 | convolution fusion | flops 406847488 | bytes 18874368 | tf_op jit(solution)/shard_map/rjpa,rjpb->rajb/dot_general | solution.py:31
  66.2 6.7 %fusion.4 = f32[64,32,128]{2,1,0:T(8,128)S(1)} fusion(f32[64,32,128]{2,1,0:T(8,128)S(1)} %bitcast.199, f32[1,128,64,128]{1,3,2,0:T(8,128)S(1)} %fusion.3), kind=kOutput, calls=%fused_computation.13 | convolution fusion | flops 402653184 | bytes 6291456 | tf_op jit(solution)/shard_map/rjpa,rajb->rjpb/dot_general | solution.py:54
  72.8 1.2 fusion.25
  74.1 1.4 gather_fusion.1
  76.2 2.3 fusion.17
  78.5 7.4 %all-to-all-start.1 = ((bf16[1,64,32,128]{3,2,0,1:T(8,128)(2,1)}), bf16[1,64,32,128]{3,2,0,1:T(8,128)(2,1)S(1)}, u32[]{:S(2)}, u32[]{:S(2)}) async-start(bf16[1,64,32,128]{3,2,0,1:T(8,128)(2,1)} %get-tuple-element.39), calls=%async_computation.1 | async-start | bytes 1048576 | tf_op jit(solution)/shard_map/all_to_all | solution.py:58
  85.9 2.2 fusion.22
  88.1 12.1 %all-to-all-done.1 = bf16[1,64,32,128]{3,2,0,1:T(8,128)(2,1)S(1)} async-done(((bf16[1,64,32,128]{3,2,0,1:T(8,128)(2,1)}), bf16[1,64,32,128]{3,2,0,1:T(8,128)(2,1)S(1)}, u32[]{:S(2)}, u32[]{:S(2)}) %all-to-all-start.1) | async-done | bytes 524320 | tf_op jit(solution)/shard_map/all_to_all | solution.py:58
  101.0 4.5 %all-to-all-start = ((bf16[1,64,32,128]{3,2,0,1:T(8,128)(2,1)}), bf16[1,64,32,128]{3,2,0,1:T(8,128)(2,1)}, u32[]{:S(2)}, u32[]{:S(2)}) async-start(bf16[1,64,32,128]{3,2,0,1:T(8,128)(2,1)} %get-tuple-element.40), calls=%async_computation | async-start | bytes 1048576 | tf_op jit(solution)/shard_map/all_to_all | solution.py:58
  105.5 8.7 %fusion = bf16[1,128,64,128]{1,3,2,0:T(8,128)(2,1)S(1)} fusion(f32[1,128,64,128]{1,3,2,0:T(8,128)} %copy-done, f32[64,32,128]{2,1,0:T(8,128)} %fusion.22, f32[64,32,128]{2,1,0:T(8,128)S(1)} %bitcast.200), kind=kOutput, calls=%fused_computation.6 | convolution fusion | flops 404750336 | bytes 8388608 | tf_op jit(solution)/shard_map/rjpa,rjpb->rajb/dot_general | solution.py:31
  114.1 2.9 %copy.51 = bf16[1,128,8192]{2,1,0:T(8,128)(2,1)} copy(bf16[1,128,8192]{1,2,0:T(8,128)(2,1)S(1)} %bitcast.210) | data formatting | bytes 4194304
  117.0 4.4 %copy.35 = f32[128,8192]{0,1:T(8,128)} copy(bf16[128,8192]{1,0:T(8,128)(2,1)} %param.9) | data formatting | bytes 6291456 | tf_op jit(solution)/shard_map/reshape | solution.py:45
  123.4 40.9 %all-reduce = (f32[]{:T(128)}, f32[]{:T(128)}) all-reduce(f32[]{:T(128)} %get-tuple-element.38, f32[]{:T(128)} %get-tuple-element.30), channel_id=1, replica_groups=mesh['wide'=16,'shard'=2] {'wide','shard'}, use_global_device_ids=true, to_apply=%region_3.5 | all-reduce | flops 2 | bytes 16 | tf_op jit(solution)/shard_map/psum | solution.py:66
  165.8 22.8 %all_gather.7 = bf16[1,64,32,128]{3,2,0,1:T(8,128)(2,1)S(1)} all-gather(bf16[1,4,32,128]{3,2,0,1:T(8,128)(2,1)S(1)} %divide_convert_fusion), channel_id=1, replica_groups=mesh['wide'=16,'shard'=2] {'wide'}, dimensions={1}, use_global_device_ids=true | all-gather | bytes 557056 | tf_op jit(solution)/shard_map/all_gather | solution.py:69
  188.8 18.9 %all_gather.6 = bf16[1,64,32,128]{3,2,0,1:T(8,128)(2,1)S(1)} all-gather(bf16[1,4,32,128]{3,2,0,1:T(8,128)(2,1)S(1)} %divide_convert_fusion.1), channel_id=1, replica_groups=mesh['wide'=16,'shard'=2] {'wide'}, dimensions={1}, use_global_device_ids=true | all-gather | bytes 557056 | tf_op jit(solution)/shard_map/all_gather | solution.py:69
  207.8 1.6 gather_fusion.4
  210.0 2.4 %fusion.8 = f32[64,32,128]{2,1,0:T(8,128)S(1)} fusion(f32[64,32,128]{2,1,0:T(8,128)} %gather_fusion.4, pred[64]{0:T(512)(128)(4,1)S(1)} %and_bitcast_fusion, f32[128]{0:T(128)S(1)} %get-tuple-element.41, f32[128]{0:T(128)S(1)} %get-tuple-element.42), kind=kOutput, calls=%fused_computation.23 | convolution fusion | flops 402964480 | bytes 2098240 | tf_op jit(solution)/shard_map/rjpc,cb->rjpb/dot_general | solution.py:30
  212.5 1.2 fusion.11
  213.7 6.7 %fusion.60 = f32[64,128,128]{2,1,0:T(8,128)S(1)} fusion(f32[64,32,128]{2,1,0:T(8,128)S(1)} %fusion.11, f32[64,32,128]{2,1,0:T(8,128)S(1)} %bitcast.201), kind=kOutput, calls=%fused_computation.104 | convolution fusion | flops 402653184 | bytes 6291456 | tf_op jit(solution)/shard_map/rjpa,rjpb->rajb/dot_general | solution.py:31
  220.4 7.4 %fusion.1 = bf16[1,128,64,128]{1,3,2,0:T(8,128)(2,1)S(1)} fusion(f32[1,128,64,128]{1,3,2,0:T(8,128)S(1)} %bitcast.203, f32[64,128,128]{2,1,0:T(8,128)S(1)} %fusion.60, f32[64,32,128]{2,1,0:T(8,128)S(1)} %fusion.8, f32[64,32,128]{2,1,0:T(8,128)S(1)} %bitcast.202), kind=kOutput, calls=%fused_computation.8 | convolution fusion | flops 407896064 | bytes 12582912 | tf_op jit(solution)/shard_map/rjpa,rjpb->rajb/dot_general | solution.py:31
  227.8 2.9 %copy.50 = bf16[128,8192]{1,0:T(8,128)(2,1)} copy(bf16[128,8192]{0,1:T(8,128)(2,1)S(1)} %bitcast.209) | data formatting | bytes 4194304
  (46 shorter events, 7.9 us)
Async XLA Ops:
  10.0 2.7 %copy-start.2 = (bf16[1,128,8192]{2,1,0:T(8,128)(2,1)S(1)}, bf16[1,128,8192]{2,1,0:T(8,128)(2,1)}, u32[]{:S(2)}) copy-start(bf16[1,128,8192]{2,1,0:T(8,128)(2,1)} %param.10) | copy-start | bytes 6291460
  66.2 7.9 %copy-start = (f32[1,128,64,128]{1,3,2,0:T(8,128)}, f32[1,128,64,128]{1,3,2,0:T(8,128)S(1)}, u32[]{:S(2)}) copy-start(f32[1,128,64,128]{1,3,2,0:T(8,128)S(1)} %fusion.3) | copy-start | bytes 12582916
  78.5 21.7 %all-to-all-start.1 = ((bf16[1,64,32,128]{3,2,0,1:T(8,128)(2,1)}), bf16[1,64,32,128]{3,2,0,1:T(8,128)(2,1)S(1)}, u32[]{:S(2)}, u32[]{:S(2)}) async-start(bf16[1,64,32,128]{3,2,0,1:T(8,128)(2,1)} %get-tuple-element.39), calls=%async_computation.1 | async-start | bytes 1048576 | tf_op jit(solution)/shard_map/all_to_all | solution.py:58
  100.2 0.8 copy-start.3
  101.0 20.5 %all-to-all-start = ((bf16[1,64,32,128]{3,2,0,1:T(8,128)(2,1)}), bf16[1,64,32,128]{3,2,0,1:T(8,128)(2,1)}, u32[]{:S(2)}, u32[]{:S(2)}) async-start(bf16[1,64,32,128]{3,2,0,1:T(8,128)(2,1)} %get-tuple-element.40), calls=%async_computation | async-start | bytes 1048576 | tf_op jit(solution)/shard_map/all_to_all | solution.py:58
  117.0 4.4 %copy-start.9 = (s32[1,64]{1,0:T(1,128)S(1)}, s32[1,64]{1,0:T(1,128)}, u32[]{:S(2)}) copy-start(s32[1,64]{1,0:T(1,128)} %param.13) | copy-start | bytes 772
  117.0 4.4 %copy-start.4 = (bf16[1,64,32,128]{3,2,0,1:T(8,128)(2,1)S(1)}, bf16[1,64,32,128]{3,2,0,1:T(8,128)(2,1)}, u32[]{:S(2)}) copy-start(bf16[1,64,32,128]{3,2,0,1:T(8,128)(2,1)} %copy-done.3) | copy-start | bytes 1572868
  117.0 5.6 %copy-start.5 = (f32[1,4,32,128]{3,2,1,0:T(8,128)S(1)}, f32[1,4,32,128]{3,2,1,0:T(8,128)}, u32[]{:S(2)}) copy-start(f32[1,4,32,128]{3,2,1,0:T(8,128)} %param.15) | copy-start | bytes 196612
  117.0 5.6 %copy-start.6 = (f32[1,4,32,128]{3,2,1,0:T(8,128)S(1)}, f32[1,4,32,128]{3,2,1,0:T(8,128)}, u32[]{:S(2)}) copy-start(f32[1,4,32,128]{3,2,1,0:T(8,128)} %param.14) | copy-start | bytes 196612
  123.4 86.6 %copy-start.7 = (f32[1,4,32,128]{3,2,0,1:T(8,128)}, f32[1,4,32,128]{3,2,0,1:T(8,128)S(1)}, u32[]{:S(2)}) copy-start(f32[1,4,32,128]{3,2,0,1:T(8,128)S(1)} %get-tuple-element.31) | copy-start | bytes 196612
  123.4 86.6 %copy-start.8 = (f32[1,4,32,128]{3,2,0,1:T(8,128)}, f32[1,4,32,128]{3,2,0,1:T(8,128)S(1)}, u32[]{:S(2)}) copy-start(f32[1,4,32,128]{3,2,0,1:T(8,128)S(1)} %get-tuple-element.32) | copy-start | bytes 196612
  212.5 8.0 %copy-start.1 = (f32[128,8192]{0,1:T(8,128)S(1)}, f32[128,8192]{0,1:T(8,128)}, u32[]{:S(2)}) copy-start(f32[128,8192]{0,1:T(8,128)} %copy.35) | copy-start | bytes 12582916
where the time goes:
time: 236 us; the launch traced here: 232 us
  blocking collectives  82.6 us (35%)
  matrix products  61.7 us (26%)
  local copies, waits for them, and re-layouts  44.2 us (19%)
  other arithmetic  16.5 us (7%)
  waiting for transfers between devices  12.1 us (5%)
  starting transfers between devices  11.9 us (5%)
  between operations  2.56 us (1%)
    all_gather x2, blocking collectives, per_device(): gathered = lax.all_gather(update, 'wide', axis=1, tiled=True)  41.7 us
    psum x1, blocking collectives, per_device(): power_sum = lax.psum(jnp.sum(raw_update * raw_update), ('wide', 'shard'))  40.9 us
    dot_general x4, matrix products, inverse(): return jnp.einsum('rjpa,rjpb->rajb', picked, right_part, precision=highest)  32.9 us
    dot_general x2, matrix products, per_device(): jnp.einsum('rjpa,rajb->rjpb', picked, blended, precision=highest)  19.4 us
    unnamed x25, local copies, waits for them, and re-layouts  12.7 us
    all_to_all x2, waiting for transfers between devices, per_device(): lax.all_to_all(slot_band.astype(jnp.bfloat16), 'wide', split_axis=1, conc...  12.1 us
    all_to_all x2, starting transfers between devices, per_device(): lax.all_to_all(slot_band.astype(jnp.bfloat16), 'wide', split_axis=1, conc...  11.9 us
    convert_element_type x2, local copies, waits for them, and re-layouts, per_device(): grads[step_index, 0].astype(jnp.float32).reshape(block_shape)  11.2 us
  transfers between devices with their start and end apart: 2, of which 1 were waited for; matrix products, arithmetic and copies ran while one was open for 8% of the time, Pallas kernels for 0%

commit v1 on v0

--- a/solution.py
+++ b/solution.py
@@ -55,8 +55,14 @@
         band_coef = jnp.einsum("rjpb,cb->rjpc", left_part, basis, precision=highest)
         moment_now = blended - inverse(band_coef, picked, basis)
         slot_band = jnp.take_along_axis(band_coef, slot_order[:, :, None, None], axis=1)
-        pieces = lax.all_to_all(
-            slot_band.astype(jnp.bfloat16), "wide", split_axis=1, concat_axis=0, tiled=True
+        pieces = jnp.concatenate(
+            lax.all_to_all(
+                jnp.stack(jnp.split(slot_band.astype(jnp.bfloat16), lax.axis_size("wide"), axis=1)),
+                "wide",
+                0,
+                0,
+            ),
+            axis=0,
         ).astype(slot_band.dtype)
         summed = jnp.sum(pieces.reshape((replicas, row_blocks) + pieces.shape[1:]), axis=0)
         mean_band = summed / replicas

time: 236 us -> 244 us (1.034)
  local copies, waits for them, and re-layouts: 44.2 us -> 63.8 us
  waiting for transfers between devices: 12.1 us -> 2.21 us
    unnamed x25 -> x55, local copies, waits for them, and re-layouts: 12.7 us -> 31 us
    all_to_all x2, waiting for transfers between devices: 12.1 us -> 2.21 us  [per_device(): lax.all_to_all(jnp.stack(jnp.split(slot_band.astype(jnp.bfloat16), lax.ax...]
  transfers between devices with their start and end apart: 2 -> 2, of which waited for: 1 -> 1; matrix products, arithmetic and copies ran while one was open for 8% -> 12% of each run, Pallas kernels for 0% -> 0%
where the time goes in v1:
time: 244 us; the launch traced here: 240 us
  blocking collectives  82.4 us (34%)
  local copies, waits for them, and re-layouts  63.8 us (26%)
  matrix products  61.7 us (25%)
  other arithmetic  15.5 us (6%)
  starting transfers between devices  11.9 us (5%)
  between operations  2.59 us (1%)
    all_gather x2, blocking collectives, per_device(): gathered = lax.all_gather(update, 'wide', axis=1, tiled=True)  41.7 us
    psum x1, blocking collectives, per_device(): power_sum = lax.psum(jnp.sum(raw_update * raw_update), ('wide', 'shard'))  40.8 us
    dot_general x4, matrix products, inverse(): return jnp.einsum('rjpa,rjpb->rajb', picked, right_part, precision=highest)  32.9 us
    unnamed x55, local copies, waits for them, and re-layouts  31 us
    dot_general x2, matrix products, per_device(): jnp.einsum('rjpa,rajb->rjpb', picked, blended, precision=highest)  19.4 us
    all_to_all x2, starting transfers between devices, per_device(): lax.all_to_all(jnp.stack(jnp.split(slot_band.astype(jnp.bfloat16), lax.ax...  11.9 us
    convert_element_type x2, local copies, waits for them, and re-layouts, per_device(): grads[step_index, 0].astype(jnp.float32).reshape(block_shape)  11.2 us
    dot_general x4, matrix products, inverse(): right_part = jnp.einsum('rjpc,cb->rjpb', coefs, basis, precision=highest)  7.04 us
  transfers between devices with their start and end apart: 2, of which 1 were waited for; matrix products, arithmetic and copies ran while one was open for 12% of the time, Pallas kernels for 0%

profile of v1, /device:TPU:0, one launch (start us, length us, event | category | flops | bytes accessed | tf_op | source)
XLA Modules:
  0.0 240.0 jit_solution(2538649339158480120)
XLA Ops:
  3.4 6.6 %slice_convert_fusion.1 = (f32[1,1,128,8192]{3,2,1,0:T(8,128)}, f32[16,8,64,128]{3,1,2,0:T(8,128)S(1)}, f32[1,1,128,8192]{3,2,1,0:T(8,128)}) fusion(bf16[2,1,128,8192]{3,2,1,0:T(8,128)(2,1)} %param.11), kind=kLoop, calls=%fused_computation.20 | loop fusion | flops 2097152 | bytes 16777216 | tf_op jit(solution)/shard_map/convert_element_type | solution.py:51
  10.0 2.7 %copy.54 = f32[16,8,64,128]{3,2,1,0:T(8,128)} copy(f32[16,8,64,128]{3,1,2,0:T(8,128)S(1)} %get-tuple-element.34) | data formatting | bytes 8388608
  12.7 2.5 %convert_multiply_fusion = (f32[1,128,8192]{2,1,0:T(8,128)}, f32[16,8,64,128]{3,1,2,0:T(8,128)S(1)}) fusion(bf16[1,128,8192]{2,1,0:T(8,128)(2,1)S(1)} %copy-done.2), kind=kLoop, calls=%fused_computation.18 | loop fusion | flops 2097152 | bytes 10485760 | tf_op jit(solution)/shard_map/mul | solution.py:51
  15.3 2.7 %copy.53 = f32[16,8,64,128]{3,2,1,0:T(8,128)} copy(f32[16,8,64,128]{3,1,2,0:T(8,128)S(1)} %get-tuple-element.37) | data formatting | bytes 8388608
  18.2 6.0 %gather_fusion = f32[2048,128]{1,0:T(8,128)S(1)} fusion(f32[128,128]{1,0:T(8,128)S(1)} %cosine_multiply_fusion, s32[2048]{0:T(1024)S(1)} %broadcast_clamp_fusion), kind=kCustom, calls=%fused_computation.4 | custom fusion | bytes 2105344 | tf_op jit(solution)/shard_map/gather | solution.py:26
  24.2 12.7 %fusion.6 = f32[64,32,128]{2,1,0:T(8,128)S(1)} fusion(f32[64,32,128]{2,1,0:T(8,128)S(1)} %bitcast.313, f32[128,64,128]{2,1,0:T(8,128)} %bitcast.320, f32[128,64,128]{2,1,0:T(8,128)} %bitcast.321), kind=kOutput, calls=%fused_computation.16 | convolution fusion | flops 403701760 | bytes 10485760 | tf_op jit(solution)/shard_map/rjpa,rajb->rjpb/dot_general | solution.py:54
  36.9 1.2 fusion.28
  38.1 1.2 fusion.25
  39.3 5.6 %copy.43 = f32[1,1,128,8192]{2,3,1,0:T(8,128)} copy(f32[1,1,128,8192]{3,2,1,0:T(8,128)} %get-tuple-element.33) | data formatting | bytes 8388608 | tf_op jit(solution)/shard_map/convert_element_type | solution.py:51
  44.9 5.6 %copy.44 = f32[1,1,128,8192]{2,3,1,0:T(8,128)} copy(f32[1,1,128,8192]{3,2,1,0:T(8,128)} %get-tuple-element.35) | data formatting | bytes 8388608 | tf_op jit(solution)/shard_map/convert_element_type | solution.py:51
  50.5 5.6 %copy.42 = f32[1,128,8192]{1,2,0:T(8,128)} copy(f32[1,128,8192]{2,1,0:T(8,128)} %get-tuple-element.36) | data formatting | bytes 8388608 | tf_op jit(solution)/shard_map/mul | solution.py:51
  56.1 10.1 %fusion.3 = f32[1,128,64,128]{1,3,2,0:T(8,128)S(1)} fusion(f32[1,128,64,128]{1,3,2,0:T(8,128)} %bitcast.323, f32[1,128,64,128]{1,3,2,0:T(8,128)} %bitcast.324, f32[1,128,64,128]{1,3,2,0:T(8,128)} %bitcast.322, f32[64,32,128]{2,1,0:T(8,128)S(1)} %fusion.25, f32[64,32,128]{2,1,0:T(8,128)S(1)} %bitcast.314), kind=kOutput, calls=%fused_computation.11 | convolution fusion | flops 406847488 | bytes 18874368 | tf_op jit(solution)/shard_map/rjpa,rjpb->rajb/dot_general | solution.py:31
  66.2 6.7 %fusion.4 = f32[64,32,128]{2,1,0:T(8,128)S(1)} fusion(f32[64,32,128]{2,1,0:T(8,128)S(1)} %bitcast.315, f32[1,128,64,128]{1,3,2,0:T(8,128)S(1)} %fusion.3), kind=kOutput, calls=%fused_computation.13 | convolution fusion | flops 402653184 | bytes 6291456 | tf_op jit(solution)/shard_map/rjpa,rajb->rjpb/dot_general | solution.py:54
  72.8 1.2 fusion.23
  74.1 1.4 gather_fusion.1
  76.2 1.3 fusion.10
  87.2 7.4 %all-to-all-start = ((bf16[16,1,4,32,128]{4,3,2,1,0:T(8,128)(2,1)}), bf16[16,1,4,32,128]{4,3,2,1,0:T(8,128)(2,1)S(1)}, u32[]{:S(2)}, u32[]{:S(2)}) async-start(bf16[16,1,4,32,128]{4,3,2,1,0:T(8,128)(2,1)} %constant_dynamic-update-slice_fusion), calls=%async_computation | async-start | bytes 1048576 | tf_op jit(solution)/shard_map/all_to_all | solution.py:59
  104.5 2.2 fusion.20
  106.7 2.2 all-to-all-done
  109.7 4.4 %all-to-all-start.1 = ((bf16[16,1,4,32,128]{4,3,2,1,0:T(8,128)(2,1)}), bf16[16,1,4,32,128]{4,3,2,1,0:T(8,128)(2,1)}, u32[]{:S(2)}, u32[]{:S(2)}) async-start(bf16[16,1,4,32,128]{4,3,2,1,0:T(8,128)(2,1)} %constant_dynamic-update-slice_fusion.16), calls=%async_computation.1 | async-start | bytes 1048576 | tf_op jit(solution)/shard_map/all_to_all | solution.py:59
  114.2 8.7 %fusion = bf16[1,128,64,128]{1,3,2,0:T(8,128)(2,1)S(1)} fusion(f32[1,128,64,128]{1,3,2,0:T(8,128)} %copy-done, f32[64,32,128]{2,1,0:T(8,128)} %fusion.20, f32[64,32,128]{2,1,0:T(8,128)S(1)} %bitcast.316), kind=kOutput, calls=%fused_computation.6 | convolution fusion | flops 404750336 | bytes 8388608 | tf_op jit(solution)/shard_map/rjpa,rjpb->rajb/dot_general | solution.py:31
  122.8 2.9 %copy.49 = bf16[1,128,8192]{2,1,0:T(8,128)(2,1)} copy(bf16[1,128,8192]{1,2,0:T(8,128)(2,1)S(1)} %bitcast.326) | data formatting | bytes 4194304
  125.8 4.4 %copy.35 = f32[128,8192]{0,1:T(8,128)} copy(bf16[128,8192]{1,0:T(8,128)(2,1)} %param.9) | data formatting | bytes 6291456 | tf_op jit(solution)/shard_map/reshape | solution.py:45
  132.1 40.8 %all-reduce = (f32[]{:T(128)}, f32[]{:T(128)}) all-reduce(f32[]{:T(128)} %get-tuple-element.38, f32[]{:T(128)} %get-tuple-element.30), channel_id=1, replica_groups=mesh['wide'=16,'shard'=2] {'wide','shard'}, use_global_device_ids=true, to_apply=%region_3.5 | all-reduce | flops 2 | bytes 16 | tf_op jit(solution)/shard_map/psum | solution.py:72
  174.3 22.8 %all_gather.7 = bf16[1,64,32,128]{3,2,0,1:T(8,128)(2,1)S(1)} all-gather(bf16[1,4,32,128]{3,2,0,1:T(8,128)(2,1)S(1)} %divide_convert_fusion), channel_id=1, replica_groups=mesh['wide'=16,'shard'=2] {'wide'}, dimensions={1}, use_global_device_ids=true | all-gather | bytes 557056 | tf_op jit(solution)/shard_map/all_gather | solution.py:75
  197.3 18.9 %all_gather.6 = bf16[1,64,32,128]{3,2,0,1:T(8,128)(2,1)S(1)} all-gather(bf16[1,4,32,128]{3,2,0,1:T(8,128)(2,1)S(1)} %divide_convert_fusion.1), channel_id=1, replica_groups=mesh['wide'=16,'shard'=2] {'wide'}, dimensions={1}, use_global_device_ids=true | all-gather | bytes 557056 | tf_op jit(solution)/shard_map/all_gather | solution.py:75
  216.3 1.6 gather_fusion.4
  218.5 2.4 %fusion.8 = f32[64,32,128]{2,1,0:T(8,128)S(1)} fusion(f32[64,32,128]{2,1,0:T(8,128)} %gather_fusion.4, pred[64]{0:T(512)(128)(4,1)S(1)} %and_bitcast_fusion, f32[128]{0:T(128)S(1)} %get-tuple-element.41, f32[128]{0:T(128)S(1)} %get-tuple-element.42), kind=kOutput, calls=%fused_computation.21 | convolution fusion | flops 402964480 | bytes 2098240 | tf_op jit(solution)/shard_map/rjpc,cb->rjpb/dot_general | solution.py:30
  221.0 1.2 fusion.11
  222.2 6.7 %fusion.58 = f32[64,128,128]{2,1,0:T(8,128)S(1)} fusion(f32[64,32,128]{2,1,0:T(8,128)S(1)} %fusion.11, f32[64,32,128]{2,1,0:T(8,128)S(1)} %bitcast.317), kind=kOutput, calls=%fused_computation.166 | convolution fusion | flops 402653184 | bytes 6291456 | tf_op jit(solution)/shard_map/rjpa,rjpb->rajb/dot_general | solution.py:31
  228.9 7.4 %fusion.1 = bf16[1,128,64,128]{1,3,2,0:T(8,128)(2,1)S(1)} fusion(f32[1,128,64,128]{1,3,2,0:T(8,128)S(1)} %bitcast.319, f32[64,128,128]{2,1,0:T(8,128)S(1)} %fusion.58, f32[64,32,128]{2,1,0:T(8,128)S(1)} %fusion.8, f32[64,32,128]{2,1,0:T(8,128)S(1)} %bitcast.318), kind=kOutput, calls=%fused_computation.8 | convolution fusion | flops 407896064 | bytes 12582912 | tf_op jit(solution)/shard_map/rjpa,rjpb->rajb/dot_general | solution.py:31
  236.3 2.9 %copy.48 = bf16[128,8192]{1,0:T(8,128)(2,1)} copy(bf16[128,8192]{0,1:T(8,128)(2,1)S(1)} %bitcast.325) | data formatting | bytes 4194304
  (78 shorter events, 27.5 us)
Async XLA Ops:
  10.0 2.7 %copy-start.2 = (bf16[1,128,8192]{2,1,0:T(8,128)(2,1)S(1)}, bf16[1,128,8192]{2,1,0:T(8,128)(2,1)}, u32[]{:S(2)}) copy-start(bf16[1,128,8192]{2,1,0:T(8,128)(2,1)} %param.10) | copy-start | bytes 6291460
  66.2 7.9 %copy-start = (f32[1,128,64,128]{1,3,2,0:T(8,128)}, f32[1,128,64,128]{1,3,2,0:T(8,128)S(1)}, u32[]{:S(2)}) copy-start(f32[1,128,64,128]{1,3,2,0:T(8,128)S(1)} %fusion.3) | copy-start | bytes 12582916
  87.2 21.7 %all-to-all-start = ((bf16[16,1,4,32,128]{4,3,2,1,0:T(8,128)(2,1)}), bf16[16,1,4,32,128]{4,3,2,1,0:T(8,128)(2,1)S(1)}, u32[]{:S(2)}, u32[]{:S(2)}) async-start(bf16[16,1,4,32,128]{4,3,2,1,0:T(8,128)(2,1)} %constant_dynamic-update-slice_fusion), calls=%async_computation | async-start | bytes 1048576 | tf_op jit(solution)/shard_map/all_to_all | solution.py:59
  108.9 0.8 copy-start.3
  109.7 20.5 %all-to-all-start.1 = ((bf16[16,1,4,32,128]{4,3,2,1,0:T(8,128)(2,1)}), bf16[16,1,4,32,128]{4,3,2,1,0:T(8,128)(2,1)}, u32[]{:S(2)}, u32[]{:S(2)}) async-start(bf16[16,1,4,32,128]{4,3,2,1,0:T(8,128)(2,1)} %constant_dynamic-update-slice_fusion.16), calls=%async_computation.1 | async-start | bytes 1048576 | tf_op jit(solution)/shard_map/all_to_all | solution.py:59
  125.7 4.4 %copy-start.9 = (s32[1,64]{1,0:T(1,128)S(1)}, s32[1,64]{1,0:T(1,128)}, u32[]{:S(2)}) copy-start(s32[1,64]{1,0:T(1,128)} %param.13) | copy-start | bytes 772
  125.7 4.4 %copy-start.4 = (bf16[16,1,4,32,128]{4,3,2,1,0:T(8,128)(2,1)S(1)}, bf16[16,1,4,32,128]{4,3,2,1,0:T(8,128)(2,1)}, u32[]{:S(2)}) copy-start(bf16[16,1,4,32,128]{4,3,2,1,0:T(8,128)(2,1)} %copy-done.3) | copy-start | bytes 1572868
  125.7 5.6 %copy-start.5 = (f32[1,4,32,128]{3,2,1,0:T(8,128)S(1)}, f32[1,4,32,128]{3,2,1,0:T(8,128)}, u32[]{:S(2)}) copy-start(f32[1,4,32,128]{3,2,1,0:T(8,128)} %param.15) | copy-start | bytes 196612
  125.7 5.6 %copy-start.6 = (f32[1,4,32,128]{3,2,1,0:T(8,128)S(1)}, f32[1,4,32,128]{3,2,1,0:T(8,128)}, u32[]{:S(2)}) copy-start(f32[1,4,32,128]{3,2,1,0:T(8,128)} %param.14) | copy-start | bytes 196612
  132.1 86.4 %copy-start.7 = (f32[1,4,32,128]{3,2,0,1:T(8,128)}, f32[1,4,32,128]{3,2,0,1:T(8,128)S(1)}, u32[]{:S(2)}) copy-start(f32[1,4,32,128]{3,2,0,1:T(8,128)S(1)} %get-tuple-element.31) | copy-start | bytes 196612
  132.1 86.4 %copy-start.8 = (f32[1,4,32,128]{3,2,0,1:T(8,128)}, f32[1,4,32,128]{3,2,0,1:T(8,128)S(1)}, u32[]{:S(2)}) copy-start(f32[1,4,32,128]{3,2,0,1:T(8,128)S(1)} %get-tuple-element.32) | copy-start | bytes 196612
  221.0 7.9 %copy-start.1 = (f32[128,8192]{0,1:T(8,128)S(1)}, f32[128,8192]{0,1:T(8,128)}, u32[]{:S(2)}) copy-start(f32[128,8192]{0,1:T(8,128)} %copy.35) | copy-start | bytes 12582916
